TPU v7x, 512 devices: a whole 4x4x16 slice. The times are simulated.
512 devices in a mesh: seq: 4 (over z_lo), fsdp: 32 (over z_hi, y, core), dp: 4 (over x).
Axes of the slice: x: 4, y: 4, z: 16 (z_hi: 4, z_lo: 4; z = z_hi * 4 + z_lo), core: 2. Of those that a mesh axis runs over, the one named last changes fastest.
Arguments:
- query: bfloat16 [128, 768, 1024], P(('fsdp', 'dp'), 'seq'), may hold values from -6 to 6
- key: bfloat16 [128, 768, 1024], P(('fsdp', 'dp'), 'seq'), may hold values from -6 to 6
- value: bfloat16 [128, 768, 1024], P(('fsdp', 'dp'), 'seq'), may hold values from -4 to 4
- out_weight: bfloat16 [1024, 2048], P('fsdp'), may hold values from -0.1875 to 0.1875
- out_grad: bfloat16 [128, 768, 2048], P(('fsdp', 'dp'), 'seq'), may hold values from -5 to 5
- block_ids: int32 [8], P('seq'), may hold values from 0 to 7, as said below
Outputs:
- query_grad: bfloat16 [128, 768, 1024], P(('fsdp', 'dp'), 'seq')
- key_grad: bfloat16 [128, 768, 1024], P(('fsdp', 'dp'), 'seq')
- value_grad: bfloat16 [128, 768, 1024], P(('fsdp', 'dp'), 'seq')
- weight_grad: bfloat16 [1024, 2048], P('fsdp')
Inputs may be any that keep to these rules, and one draw needn't show every extreme that they name: `block_ids`: each number 0 to 7 appears once, and entries 2 i and 2 i + 1 always sum to 7.
All inputs are finite; a program needn't handle non-finite values.
Results may differ from a plain program's by a relative error of at most 0.027.
Values may be sent and summed in bfloat16 or wider, within the bound.
No kernel may reach another device: no remote copies, remote signals or barrier semaphores. Data moves between devices by JAX's collectives and lax.ppermute only.
A program may use at most 64 MiB of HBM per device.

v0:
```python
import math
import jax
import jax.numpy as jnp
from jax import lax
from jax.sharding import PartitionSpec as P

HEADS = 8
HD = 128


def positions_of(block_list, block_rows):
    offsets = jnp.arange(block_rows, dtype=jnp.int32)
    return (block_list[:, None] * block_rows + offsets[None, :]).reshape(-1)


def shards(query, key, value, out_weight, out_grad, block_ids):
    tokens_here = query.shape[1]
    width_heads = query.shape[2]
    block_rows = tokens_here // block_ids.shape[0]
    score_scale = 1.0 / math.sqrt(HD)
    all_blocks = lax.all_gather(block_ids, "seq", axis=0, tiled=True)
    query_pos = positions_of(block_ids, block_rows)
    every_pos = positions_of(all_blocks, block_rows)
    key_all, value_all = (
        lax.all_gather(key, "seq", axis=1, tiled=True),
        lax.all_gather(value, "seq", axis=1, tiled=True),
    )
    query_heads = query[0].reshape(tokens_here, HEADS, HD)
    key_heads = key_all[0].reshape(-1, HEADS, HD)
    value_heads = value_all[0].reshape(-1, HEADS, HD)
    scores = (
        jnp.einsum("thd,khd->htk", query_heads, key_heads, preferred_element_type=jnp.float32)
        * score_scale
    )
    allowed = every_pos[None, :] <= query_pos[:, None]
    scores = jnp.where(allowed[None], scores, -jnp.inf)
    row_top = jnp.max(scores, axis=2, keepdims=True)
    row_total = jnp.sum(jnp.exp(scores - row_top), axis=2, keepdims=True)
    log_total = row_top + jnp.log(row_total)
    weights = jnp.exp(scores - log_total)
    weights_low = weights.astype(jnp.bfloat16)
    attended = jnp.einsum(
        "htk,khd->thd", weights_low, value_heads, preferred_element_type=jnp.float32
    ).astype(jnp.bfloat16)
    grad_rows = out_grad[0]
    attn_grad = lax.dot_general(
        grad_rows,
        lax.all_gather(out_weight, "fsdp", axis=0, tiled=True),
        (((1,), (1,)), ((), ())),
        preferred_element_type=jnp.float32,
    ).astype(jnp.bfloat16)
    attended_flat = attended.reshape(tokens_here, width_heads)
    weight_shard = lax.psum_scatter(
        lax.dot_general(
            attended_flat, grad_rows, (((0,), (0,)), ((), ())), preferred_element_type=jnp.float32
        ).astype(jnp.bfloat16),
        "fsdp",
        scatter_dimension=0,
        tiled=True,
    ).astype(jnp.float32)
    token_count = tokens_here * lax.axis_size("seq") * lax.axis_size("fsdp") * lax.axis_size("dp")
    weight_grad = (lax.psum(weight_shard, ("seq", "dp")) * (1.0 / math.sqrt(token_count))).astype(
        jnp.bfloat16
    )
    grad_heads = attn_grad.reshape(tokens_here, HEADS, HD)
    row_delta = jnp.einsum("thd,thd->ht", grad_heads, attended, preferred_element_type=jnp.float32)
    prob_grad = jnp.einsum(
        "thd,khd->htk", grad_heads, value_heads, preferred_element_type=jnp.float32
    )
    score_grad = (weights * (prob_grad - row_delta[:, :, None])).astype(jnp.bfloat16)
    query_grad = (
        jnp.einsum("htk,khd->thd", score_grad, key_heads, preferred_element_type=jnp.float32)
        * score_scale
    ).astype(jnp.bfloat16)
    query_all, grad_all = (
        lax.all_gather(query, "seq", axis=1, tiled=True),
        lax.all_gather(attn_grad[None], "seq", axis=1, tiled=True),
    )
    totals_all, deltas_all = (
        lax.all_gather(log_total[:, :, 0][None], "seq", axis=2, tiled=True),
        lax.all_gather(row_delta[None], "seq", axis=2, tiled=True),
    )
    local_keys = key[0].reshape(tokens_here, HEADS, HD)
    local_values = value[0].reshape(tokens_here, HEADS, HD)
    gathered_queries = query_all[0].reshape(-1, HEADS, HD)
    gathered_grads = grad_all[0].reshape(-1, HEADS, HD)
    back_scores = (
        jnp.einsum("khd,qhd->hkq", local_keys, gathered_queries, preferred_element_type=jnp.float32)
        * score_scale
    )
    back_allowed = query_pos[:, None] <= every_pos[None, :]
    back_scores = jnp.where(back_allowed[None], back_scores, -jnp.inf)
    back_weights = jnp.exp(back_scores - totals_all[0][:, None, :])
    back_low = back_weights.astype(jnp.bfloat16)
    back_prob_grad = jnp.einsum(
        "qhd,khd->hkq", gathered_grads, local_values, preferred_element_type=jnp.float32
    )
    back_score_grad = (back_weights * (back_prob_grad - deltas_all[0][:, None, :])).astype(
        jnp.bfloat16
    )
    key_grad = (
        jnp.einsum(
            "hkq,qhd->khd", back_score_grad, gathered_queries, preferred_element_type=jnp.float32
        )
        * score_scale
    ).astype(jnp.bfloat16)
    value_grad = jnp.einsum(
        "hkq,qhd->khd", back_low, gathered_grads, preferred_element_type=jnp.float32
    ).astype(jnp.bfloat16)
    return (
        query_grad.reshape(tokens_here, width_heads)[None],
        key_grad.reshape(tokens_here, width_heads)[None],
        value_grad.reshape(tokens_here, width_heads)[None],
        weight_grad,
    )


def solution(mesh):
    in_specs = (
        P(("fsdp", "dp"), "seq", None),
        P(("fsdp", "dp"), "seq", None),
        P(("fsdp", "dp"), "seq", None),
        P("fsdp", None),
        P(("fsdp", "dp"), "seq", None),
        P("seq"),
    )
    out_specs = (
        P(("fsdp", "dp"), "seq", None),
        P(("fsdp", "dp"), "seq", None),
        P(("fsdp", "dp"), "seq", None),
        P("fsdp", None),
    )
    return jax.shard_map(shards, mesh=mesh, in_specs=in_specs, out_specs=out_specs, check_vma=False)
```

profile of v0, /device:TPU:16, one launch (start us, length us, event | category | flops | bytes accessed | tf_op | source)
XLA Modules:
  0.0 531.4 jit_solution(5790894048885190867)
XLA Ops:
  7.2 0.0 copy-start
  7.2 0.0 all-gather.13.cloned.1.call-start
  7.2 0.7 all-gather.13.cloned.1.call-update
  7.9 0.0 all-gather.11.cloned.1.call-start
  8.0 0.7 all-gather.11.cloned.1.call-update
  8.7 0.0 all-gather.15.cloned.1.call-start
  8.7 0.7 all-gather.15.cloned.1.call-update
  9.4 0.0 all-gather.17.cloned.1.call-start
  9.4 0.5 all-gather.17.cloned.1.call-update
  10.0 0.0 all-gather.19.cloned.1.call-start
  10.0 1.3 dynamic-slice
  12.0 0.9 dynamic-update-slice
  12.8 9.1 %all-reduce = s32[8]{0:T(128)S(1)} all-reduce(s32[8]{0:T(128)S(1)} %dynamic-update-slice), channel_id=1, replica_groups=mesh['seq'=4,'fsdp'=32,'dp'=4] {'seq'}, use_global_device_ids=true, to_apply=%add | all-reduce | flops 8 | bytes 64
  21.9 0.1 iota_add_fusion
  22.0 0.1 add.65
  22.1 0.7 broadcast_multiply_fusion
  22.8 0.1 iota_add_fusion.1
  22.8 0.1 add.69
  22.9 1.1 copy.64
  24.0 86.7 %all-gather.13.cloned.1.call-done = bf16[1024,2048]{1,0:T(8,128)(2,1)} async-done(((bf16[32,2048]{1,0:T(8,128)(2,1)}), bf16[1024,2048]{1,0:T(8,128)(2,1)}) %all-gather.13.cloned.1.call-update) | async-done | bytes 4194320 | tf_op jit(solution)/shard_map/all_gather | solution.py:48
  110.6 0.0 copy-done
  110.6 4.5 convolution_convert_fusion.1
  115.1 0.0 all-gather.19.cloned.1.call-update
  115.1 0.0 reduce-scatter.2.cloned.1.call-start
  115.2 0.2 broadcast_compare_fusion
  115.4 39.8 %all-gather.11.cloned.1.call-done = bf16[1,768,1024]{2,1,0:T(8,128)(2,1)} async-done(((bf16[1,192,1024]{2,1,0:T(8,128)(2,1)}), bf16[1,768,1024]{2,1,0:T(8,128)(2,1)}) %all-gather.11.cloned.1.call-update) | async-done | bytes 1572880 | tf_op jit(solution)/shard_map/all_gather | solution.py:25
  155.2 1.7 copy.28
  156.9 0.0 copy-start.2
  157.0 46.7 %all-gather.15.cloned.1.call-done = bf16[1,768,1024]{2,1,0:T(8,128)(2,1)} async-done(((bf16[1,192,1024]{2,1,0:T(8,128)(2,1)}), bf16[1,768,1024]{2,1,0:T(8,128)(2,1)}) %all-gather.15.cloned.1.call-update) | async-done | bytes 1572880 | tf_op jit(solution)/shard_map/all_gather | solution.py:26
  203.7 2.6 copy.31
  206.3 1.0 fusion.3
  207.3 1.2 exponential_reduce_fusion
  208.6 0.1 copy.65
  208.6 0.1 bitcast_convert_fusion
  208.7 1.1 copy-done.3
  209.9 1.6 multiply_reduce_fusion
  211.5 0.0 copy-done.1
  211.5 0.0 copy-start.4
  211.5 0.0 copy-start.5
  211.6 3.4 convolution_convert_fusion
  214.9 0.0 reduce-scatter.2.cloned.1.call-update
  215.0 0.1 copy.66
  215.0 0.8 copy.67
  215.9 13.1 %all-gather.3 = f32[4,192,8]{1,2,0:T(8,128)S(1)} all-gather(f32[1,192,8]{1,2,0:T(8,128)S(1)} %bitcast.115), channel_id=2, replica_groups=mesh['seq'=4,'fsdp'=32,'dp'=4] {'seq'}, dimensions={0}, use_global_device_ids=true | all-gather | bytes 30720 | tf_op jit(solution)/shard_map/all_gather | solution.py:80
  229.0 0.1 reshape.140
  229.1 22.9 %all-gather.17.cloned.1.call-done = bf16[1,768,1024]{2,1,0:T(8,128)(2,1)} async-done(((bf16[1,192,1024]{2,1,0:T(8,128)(2,1)}), bf16[1,768,1024]{2,1,0:T(8,128)(2,1)}) %all-gather.17.cloned.1.call-update) | async-done | bytes 1572880 | tf_op jit(solution)/shard_map/all_gather | solution.py:76
  252.0 1.7 copy.37
  253.7 2.9 fusion.72
  256.7 6.3 %fusion.56 = bf16[192,8,128]{2,0,1:T(8,128)(2,1)} fusion(bf16[768,8,128]{0,2,1:T(8,128)(2,1)} %bitcast.105, f32[8,192,768]{2,1,0:T(8,128)} %copy-done.1, f32[8,192]{1,0:T(8,128)S(1)} %get-tuple-element.8, f32[8,192]{1,0:T(8,128)S(1)} %log_add_fusion, pred[192,768]{1,0:T(8,128)(4,1)S(1)} %get-tuple-element.5, bf16[768,8,128]{0,2,1:T(8,128)(2,1)} %bitcast.106, ...), kind=kOutput, calls=%fused_computation.39 | convolution fusion | flops 611450880 | bytes 8810496 | tf_op jit(solution)/shard_map/htk,khd->thd/dot_general | solution.py:72
  262.9 1.3 copy.36
  264.2 0.9 broadcast_in_dim_reshape.6
  265.1 13.4 %all-gather.4 = f32[4,192,8]{1,2,0:T(8,128)S(1)} all-gather(f32[1,192,8]{1,2,0:T(8,128)S(1)} %bitcast.119), channel_id=4, replica_groups=mesh['seq'=4,'fsdp'=32,'dp'=4] {'seq'}, dimensions={0}, use_global_device_ids=true | all-gather | bytes 30720 | tf_op jit(solution)/shard_map/all_gather | solution.py:81
  278.5 0.1 reshape.142
  278.6 22.4 %all-gather.19.cloned.1.call-done = bf16[768,1024]{1,0:T(8,128)(2,1)} async-done(((bf16[192,1024]{1,0:T(8,128)(2,1)}), bf16[768,1024]{1,0:T(8,128)(2,1)}) %all-gather.19.cloned.1.call-update) | async-done | bytes 1572880 | tf_op jit(solution)/shard_map/all_gather | solution.py:77
  301.0 0.0 copy-done.7
  301.0 4.8 fusion.51
  305.8 0.3 copy.45
  306.1 0.9 broadcast_in_dim_reshape.14
  307.0 4.2 fusion.57
  311.3 0.3 copy.47
  311.5 0.9 broadcast_in_dim_reshape.15
  312.4 129.9 %reduce-scatter.2.cloned.1.call-done = bf16[32,2048]{1,0:T(8,128)(2,1)} async-done(((bf16[1024,2048]{1,0:T(8,128)(2,1)}), bf16[32,2048]{1,0:T(8,128)(2,1)}) %reduce-scatter.2.cloned.1.call-update) | async-done | bytes 131088 | tf_op jit(solution)/shard_map/reduce_scatter | solution.py:53
  442.3 81.5 %all-reduce.2 = f32[32,2048]{1,0:T(8,128)S(1)} all-reduce(bf16[32,2048]{1,0:T(8,128)(2,1)} %reduce-scatter.2.cloned.1.call-done), channel_id=1, replica_groups=mesh['seq'=4,'fsdp'=32,'dp'=4] {'seq','dp'}, use_global_device_ids=true, to_apply=%region_3.4 | all-reduce | flops 65536 | bytes 393216 | tf_op jit(solution)/shard_map/psum | solution.py:62
  523.9 0.7 multiply_convert_fusion.8
  (13 shorter events, 0.1 us)
Async XLA Ops:
  7.2 103.5 %copy-start = (bf16[1,192,2048]{2,1,0:T(8,128)(2,1)S(1)}, bf16[1,192,2048]{2,1,0:T(8,128)(2,1)}, u32[]{:S(2)}) copy-start(bf16[1,192,2048]{2,1,0:T(8,128)(2,1)} %param.10) | copy-start | bytes 2359300
  7.2 103.5 %all-gather.13.cloned.1.call-start = ((), (), s32[]{:S(2)}) async-start(), calls=%async_computation.2 | async-start | bytes 4325376 | tf_op jit(solution)/shard_map/all_gather | solution.py:48
  7.9 147.3 %all-gather.11.cloned.1.call-start = ((), (), s32[]{:S(2)}) async-start(), calls=%async_computation.1 | async-start | bytes 1966080 | tf_op jit(solution)/shard_map/all_gather | solution.py:25
  8.7 195.0 %all-gather.15.cloned.1.call-start = ((), (), s32[]{:S(2)}) async-start(), calls=%async_computation.3 | async-start | bytes 1966080 | tf_op jit(solution)/shard_map/all_gather | solution.py:26
  9.4 242.6 %all-gather.17.cloned.1.call-start = ((), (), s32[]{:S(2)}) async-start(), calls=%async_computation.4 | async-start | bytes 1966080 | tf_op jit(solution)/shard_map/all_gather | solution.py:76
  10.0 291.0 %all-gather.19.cloned.1.call-start = ((), (), s32[]{:S(2)}) async-start(), calls=%async_computation.6 | async-start | bytes 1966080 | tf_op jit(solution)/shard_map/all_gather | solution.py:77
  115.1 327.2 %reduce-scatter.2.cloned.1.call-start = ((), (), s32[]{:S(2)}) async-start(), calls=%async_computation.5 | async-start | bytes 4325376 | tf_op jit(solution)/shard_map/reduce_scatter | solution.py:53
  156.9 50.3 %copy-start.2 = (bf16[1,768,1024]{1,2,0:T(8,128)(2,1)}, bf16[1,768,1024]{1,2,0:T(8,128)(2,1)S(1)}, u32[]{:S(2)}) copy-start(bf16[1,768,1024]{1,2,0:T(8,128)(2,1)S(1)} %copy.28) | copy-start | bytes 4718596
  206.3 2.3 copy-start.6
  207.3 4.2 copy-start.1
  207.3 2.6 copy-start.3
  211.5 3.4 copy-start.4
  211.5 3.5 copy-start.5
  256.7 44.3 %copy-start.7 = (bf16[24,8,8,128]{3,2,1,0:T(8,128)(2,1)S(1)}, bf16[24,8,8,128]{3,2,1,0:T(8,128)(2,1)}, u32[]{:S(2)}) copy-start(bf16[24,8,8,128]{3,2,1,0:T(8,128)(2,1)} %copy.67) | copy-start | bytes 1179652
Sparse Core Ops, SparseCore 0:
  11.1 99.4 all-gather.12
  112.7 42.4 all-gather.10
  157.3 46.2 all-gather.14
  205.6 46.3 all-gather.16
  254.5 46.4 all-gather.18
  305.4 136.9 reduce-scatter.1
where the time goes:
time: 532 us; the launch traced here: 531 us
  waiting for transfers between devices  351 us (66%)
  blocking collectives  117 us (22%)
  matrix products  28.8 us (5%)
  local copies, waits for them, and re-layouts  16.2 us (3%)
  between operations  15 us (3%)
    reduce_scatter x1, waiting for transfers between devices, shards(): lax.psum_scatter(lax.dot_general(attended_flat, grad_rows, (((0,), (0,)),...  130 us
    all_gather x1, waiting for transfers between devices, shards(): lax.all_gather(out_weight, 'fsdp', axis=0, tiled=True)  86.7 us
    psum x1, blocking collectives, shards(): lax.psum(weight_shard, ('seq', 'dp')) * (1.0 / math.sqrt(token_count))  81.5 us
    all_gather x1, waiting for transfers between devices, shards(): lax.all_gather(value, 'seq', axis=1, tiled=True)  46.7 us
    all_gather x1, waiting for transfers between devices, shards(): lax.all_gather(key, 'seq', axis=1, tiled=True)  39.8 us
    all_gather x1, waiting for transfers between devices, shards(): lax.all_gather(query, 'seq', axis=1, tiled=True)  22.9 us
    all_gather x1, waiting for transfers between devices, shards(): lax.all_gather(attn_grad[None], 'seq', axis=1, tiled=True)  22.4 us
    all_gather x1, blocking collectives, shards(): lax.all_gather(row_delta[None], 'seq', axis=2, tiled=True)  13.4 us
  transfers between devices with their start and end apart: 6, of which 6 were waited for; matrix products, arithmetic and copies ran while one was open for 9% of the time, Pallas kernels for 0%

commit v1 on v0

--- a/solution.py
+++ b/solution.py
@@ -72,9 +72,16 @@
         jnp.einsum("htk,khd->thd", score_grad, key_heads, preferred_element_type=jnp.float32)
         * score_scale
     ).astype(jnp.bfloat16)
+
+    def tell_the_plate(field):
+        return jnp.concatenate(
+            lax.all_to_all(jnp.stack([field for _ in range(lax.axis_size("seq"))], 0), "seq", 0, 0),
+            1,
+        )
+
     query_all, grad_all = (
         lax.all_gather(query, "seq", axis=1, tiled=True),
-        lax.all_gather(attn_grad[None], "seq", axis=1, tiled=True),
+        tell_the_plate(attn_grad[None]),
     )
     totals_all, deltas_all = (
         lax.all_gather(log_total[:, :, 0][None], "seq", axis=2, tiled=True),

time: 532 us -> 511 us (0.961)
  the two profiles are of different devices: /device:TPU:16 before, /device:TPU:8 now
where the time goes in v1:
time: 511 us
  waiting for transfers between devices  264 us (52%)
  blocking collectives  169 us (33%)
  matrix products  33.6 us (7%)
  local copies, waits for them, and re-layouts  18.6 us (4%)
  between operations  14.6 us (3%)
  other arithmetic  6.07 us (1%)
    all_gather x1, waiting for transfers between devices, shards(): lax.all_gather(out_weight, 'fsdp', axis=0, tiled=True)  91.5 us
    reduce_scatter x1, waiting for transfers between devices, shards(): lax.psum_scatter(lax.dot_general(attended_flat, grad_rows, (((0,), (0,)),...  90.3 us
    psum x1, blocking collectives, shards(): lax.psum(weight_shard, ('seq', 'dp')) * (1.0 / math.sqrt(token_count))  81.2 us
    all_gather x1, blocking collectives, shards(): lax.all_gather(log_total[:, :, 0][None], 'seq', axis=2, tiled=True)  65.9 us
    all_gather x1, waiting for transfers between devices, shards(): lax.all_gather(value, 'seq', axis=1, tiled=True)  43.6 us
    all_gather x1, waiting for transfers between devices, shards(): lax.all_gather(key, 'seq', axis=1, tiled=True)  36.5 us
    all_gather x1, blocking collectives, shards(): lax.all_gather(row_delta[None], 'seq', axis=2, tiled=True)  13.1 us
  transfers between devices with their start and end apart: 6, of which 4 were waited for; matrix products, arithmetic and copies ran while one was open for 11% of the time, Pallas kernels for 0%

profile of v1, /device:TPU:8, one launch (start us, length us, event | category | flops | bytes accessed | tf_op | source)
XLA Modules:
  0.0 510.7 jit_solution(646828153914604682)
XLA Ops:
  7.2 0.0 copy-start
  7.2 0.0 all-gather.9.cloned.1.call-start
  7.2 0.7 all-gather.9.cloned.1.call-update
  7.9 0.0 all-gather.13.cloned.1.call-start
  8.0 0.7 all-gather.13.cloned.1.call-update
  8.7 0.0 all-gather.11.cloned.1.call-start
  8.7 0.7 all-gather.11.cloned.1.call-update
  9.4 0.0 all-gather.15.cloned.1.call-start
  9.4 0.5 all-gather.15.cloned.1.call-update
  10.0 0.0 reduce-scatter.2.cloned.1.call-start
  10.0 1.3 dynamic-slice
  12.0 0.9 dynamic-update-slice
  12.8 0.7 broadcast_multiply_fusion
  13.5 9.1 %all-reduce = s32[8]{0:T(128)S(1)} all-reduce(s32[8]{0:T(128)S(1)} %dynamic-update-slice), channel_id=1, replica_groups=mesh['seq'=4,'fsdp'=32,'dp'=4] {'seq'}, use_global_device_ids=true, to_apply=%add | all-reduce | flops 8 | bytes 64
  22.6 0.1 iota_add_fusion
  22.7 0.1 add.65
  22.8 0.1 iota_add_fusion.1
  22.8 0.1 add.69
  22.9 1.1 copy.62
  24.0 0.9 broadcast_compare_fusion
  24.9 36.5 %all-gather.9.cloned.1.call-done = bf16[1,768,1024]{2,1,0:T(8,128)(2,1)} async-done(((bf16[1,192,1024]{2,1,0:T(8,128)(2,1)}), bf16[1,768,1024]{2,1,0:T(8,128)(2,1)}) %all-gather.9.cloned.1.call-update) | async-done | bytes 1572880 | tf_op jit(solution)/shard_map/all_gather | solution.py:25
  61.4 1.7 copy.27
  63.1 0.0 copy-start.1
  63.1 3.0 fusion.3
  66.1 43.6 %all-gather.13.cloned.1.call-done = bf16[1,768,1024]{2,1,0:T(8,128)(2,1)} async-done(((bf16[1,192,1024]{2,1,0:T(8,128)(2,1)}), bf16[1,768,1024]{2,1,0:T(8,128)(2,1)}) %all-gather.13.cloned.1.call-update) | async-done | bytes 1572880 | tf_op jit(solution)/shard_map/all_gather | solution.py:26
  109.8 2.6 copy.30
  112.4 0.0 copy-done.1
  112.4 3.6 exponential_reduce_fusion
  116.0 91.5 %all-gather.11.cloned.1.call-done = bf16[1024,2048]{1,0:T(8,128)(2,1)} async-done(((bf16[32,2048]{1,0:T(8,128)(2,1)}), bf16[1024,2048]{1,0:T(8,128)(2,1)}) %all-gather.11.cloned.1.call-update) | async-done | bytes 4194320 | tf_op jit(solution)/shard_map/all_gather | solution.py:48
  207.5 3.7 convolution_convert_fusion.1
  211.2 0.0 copy-start.6
  211.2 0.1 copy.63
  211.3 0.1 bitcast_convert_fusion
  211.4 3.9 multiply_reduce_fusion
  215.2 3.4 convolution_convert_fusion
  218.6 0.0 reduce-scatter.2.cloned.1.call-update
  218.7 0.0 copy-done.6
  218.7 1.4 stack.3
  220.0 3.8 all-to-all-start
  223.8 0.1 copy.64
  223.9 0.8 copy.66
  224.7 65.9 %all-gather.2 = f32[4,192,8]{1,2,0:T(8,128)S(1)} all-gather(f32[1,192,8]{1,2,0:T(8,128)S(1)} %bitcast.98), channel_id=2, replica_groups=mesh['seq'=4,'fsdp'=32,'dp'=4] {'seq'}, dimensions={0}, use_global_device_ids=true | all-gather | bytes 30720 | tf_op jit(solution)/shard_map/all_gather | solution.py:87
  290.6 0.7 reshape.140
  291.3 2.6 copy.36
  293.9 4.4 fusion.69
  298.3 0.0 copy-done.7
  298.3 5.6 %fusion.53 = bf16[192,8,128]{2,0,1:T(8,128)(2,1)S(1)} fusion(bf16[768,8,128]{0,2,1:T(8,128)(2,1)} %bitcast.86, f32[8,192,768]{2,1,0:T(8,128)} %get-tuple-element.7, f32[8,192]{1,0:T(8,128)S(1)} %get-tuple-element.8, f32[8,192]{1,0:T(8,128)S(1)} %log_add_fusion, pred[192,768]{1,0:T(8,128)(4,1)S(1)} %copy-done.9, bf16[768,8,128]{0,2,1:T(8,128)(2,1)} %bitcast.87, ...), kind=kOutput, calls=%fused_computation.37 | convolution fusion | flops 611450880 | bytes 8810496 | tf_op jit(solution)/shard_map/htk,khd->thd/dot_general | solution.py:72
  303.9 0.0 copy-start.10
  303.9 0.3 copy.35
  304.2 0.9 broadcast_in_dim_reshape.6
  305.1 13.1 %all-gather.3 = f32[4,192,8]{1,2,0:T(8,128)S(1)} all-gather(f32[1,192,8]{1,2,0:T(8,128)S(1)} %bitcast.102), channel_id=3, replica_groups=mesh['seq'=4,'fsdp'=32,'dp'=4] {'seq'}, dimensions={0}, use_global_device_ids=true | all-gather | bytes 30720 | tf_op jit(solution)/shard_map/all_gather | solution.py:88
  318.2 0.1 reshape.142
  318.3 0.0 all-to-all-done
  318.3 1.6 copy.65
  319.9 0.0 copy-done.10
  319.9 5.7 %fusion.48 = bf16[192,8,128]{2,0,1:T(8,128)(2,1)S(1)} fusion(bf16[768,8,128]{0,2,1:T(8,128)(2,1)} %bitcast.84, f32[8,192,768]{2,1,0:T(8,128)} %fusion.69, f32[8,768]{1,0:T(8,128)S(1)} %bitcast.101, f32[8,768]{1,0:T(8,128)} %bitcast.99, pred[192,768]{1,0:T(8,128)(4,1)} %get-tuple-element.4, bf16[768,8,128]{2,1,0:T(8,128)(2,1)} %bitcast.89, ...), kind=kOutput, calls=%fused_computation.36 | convolution fusion | flops 611450880 | bytes 8847360 | tf_op jit(solution)/shard_map/hkq,qhd->khd/dot_general | solution.py:109
  325.7 0.3 copy.44
  325.9 0.9 broadcast_in_dim_reshape.14
  326.9 3.9 fusion.54
  330.8 0.3 copy.46
  331.0 0.9 broadcast_in_dim_reshape.15
  331.9 90.3 %reduce-scatter.2.cloned.1.call-done = bf16[32,2048]{1,0:T(8,128)(2,1)} async-done(((bf16[1024,2048]{1,0:T(8,128)(2,1)}), bf16[32,2048]{1,0:T(8,128)(2,1)}) %reduce-scatter.2.cloned.1.call-update) | async-done | bytes 131088 | tf_op jit(solution)/shard_map/reduce_scatter | solution.py:53
  422.2 81.2 %all-reduce.2 = f32[32,2048]{1,0:T(8,128)S(1)} all-reduce(bf16[32,2048]{1,0:T(8,128)(2,1)} %reduce-scatter.2.cloned.1.call-done), channel_id=1, replica_groups=mesh['seq'=4,'fsdp'=32,'dp'=4] {'seq','dp'}, use_global_device_ids=true, to_apply=%region_3.4 | all-reduce | flops 65536 | bytes 393216 | tf_op jit(solution)/shard_map/psum | solution.py:62
  503.5 0.7 multiply_convert_fusion.8
  (20 shorter events, 0.1 us)
Async XLA Ops:
  7.2 200.3 %copy-start = (bf16[1,192,2048]{2,1,0:T(8,128)(2,1)S(1)}, bf16[1,192,2048]{2,1,0:T(8,128)(2,1)}, u32[]{:S(2)}) copy-start(bf16[1,192,2048]{2,1,0:T(8,128)(2,1)} %param.10) | copy-start | bytes 2359300
  7.2 54.2 %all-gather.9.cloned.1.call-start = ((), (), s32[]{:S(2)}) async-start(), calls=%async_computation.2 | async-start | bytes 1966080 | tf_op jit(solution)/shard_map/all_gather | solution.py:25
  7.9 101.9 %all-gather.13.cloned.1.call-start = ((), (), s32[]{:S(2)}) async-start(), calls=%async_computation.4 | async-start | bytes 1966080 | tf_op jit(solution)/shard_map/all_gather | solution.py:26
  8.7 198.8 %all-gather.11.cloned.1.call-start = ((), (), s32[]{:S(2)}) async-start(), calls=%async_computation.3 | async-start | bytes 4325376 | tf_op jit(solution)/shard_map/all_gather | solution.py:48
  9.4 281.9 %all-gather.15.cloned.1.call-start = ((), (), s32[]{:S(2)}) async-start(), calls=%async_computation.5 | async-start | bytes 1966080 | tf_op jit(solution)/shard_map/all_gather | solution.py:83
  10.0 412.3 %reduce-scatter.2.cloned.1.call-start = ((), (), s32[]{:S(2)}) async-start(), calls=%async_computation.6 | async-start | bytes 4325376 | tf_op jit(solution)/shard_map/reduce_scatter | solution.py:53
  24.9 186.5 %copy-start.8 = (pred[192,768]{1,0:T(8,128)(4,1)}, pred[192,768]{1,0:T(8,128)(4,1)S(1)}, u32[]{:S(2)}) copy-start(pred[192,768]{1,0:T(8,128)(4,1)S(1)} %get-tuple-element.5) | copy-start | bytes 442372
  63.1 49.3 %copy-start.1 = (bf16[1,768,1024]{1,2,0:T(8,128)(2,1)}, bf16[1,768,1024]{1,2,0:T(8,128)(2,1)S(1)}, u32[]{:S(2)}) copy-start(bf16[1,768,1024]{1,2,0:T(8,128)(2,1)S(1)} %copy.27) | copy-start | bytes 4718596
  116.0 95.4 %copy-start.2 = (bf16[1,768,1024]{1,2,0:T(8,128)(2,1)S(1)}, bf16[1,768,1024]{1,2,0:T(8,128)(2,1)}, u32[]{:S(2)}) copy-start(bf16[1,768,1024]{1,2,0:T(8,128)(2,1)} %copy.30) | copy-start | bytes 4718596
  211.2 7.5 %copy-start.6 = (bf16[192,1024]{1,0:T(8,128)(2,1)}, bf16[192,1024]{1,0:T(8,128)(2,1)S(1)}, u32[]{:S(2)}) copy-start(bf16[192,1024]{1,0:T(8,128)(2,1)S(1)} %convolution_convert_fusion.1) | copy-start | bytes 1179652
  218.6 5.2 %copy-start.4 = (bf16[1,192,1024]{2,1,0:T(8,128)(2,1)S(1)}, bf16[1,192,1024]{2,1,0:T(8,128)(2,1)}, u32[]{:S(2)}) copy-start(bf16[1,192,1024]{2,1,0:T(8,128)(2,1)} %param.7) | copy-start | bytes 1179652
  218.6 5.3 %copy-start.5 = (bf16[1,192,1024]{2,1,0:T(8,128)(2,1)S(1)}, bf16[1,192,1024]{2,1,0:T(8,128)(2,1)}, u32[]{:S(2)}) copy-start(bf16[1,192,1024]{2,1,0:T(8,128)(2,1)} %param.8) | copy-start | bytes 1179652
  220.0 98.3 %all-to-all-start = ((bf16[4,1,192,1024]{3,2,1,0:T(8,128)(2,1)}), bf16[4,1,192,1024]{3,2,1,0:T(8,128)(2,1)S(1)}, u32[]{:S(2)}, u32[]{:S(2)}) async-start(bf16[4,1,192,1024]{3,2,1,0:T(8,128)(2,1)} %stack.3), calls=%async_computation | async-start | bytes 3145728 | tf_op jit(solution)/shard_map/all_to_all | solution.py:78
  291.3 7.0 %copy-start.7 = (bf16[192,1024]{1,0:T(8,128)(2,1)S(1)}, bf16[192,1024]{1,0:T(8,128)(2,1)}, u32[]{:S(2)}) copy-start(bf16[192,1024]{1,0:T(8,128)(2,1)} %copy-done.6) | copy-start | bytes 1179652
  291.3 7.0 %copy-start.9 = (pred[192,768]{1,0:T(8,128)(4,1)S(1)}, pred[192,768]{1,0:T(8,128)(4,1)}, u32[]{:S(2)}) copy-start(pred[192,768]{1,0:T(8,128)(4,1)} %copy-done.8) | copy-start | bytes 442372
  303.9 16.0 %copy-start.10 = (bf16[24,8,8,128]{3,2,1,0:T(8,128)(2,1)S(1)}, bf16[24,8,8,128]{3,2,1,0:T(8,128)(2,1)}, u32[]{:S(2)}) copy-start(bf16[24,8,8,128]{3,2,1,0:T(8,128)(2,1)} %copy.66) | copy-start | bytes 1179652
  319.9 6.9 %copy-start.3 = (bf16[96,8,8,128]{3,2,1,0:T(8,128)(2,1)S(1)}, bf16[96,8,8,128]{3,2,1,0:T(8,128)(2,1)}, u32[]{:S(2)}) copy-start(bf16[96,8,8,128]{3,2,1,0:T(8,128)(2,1)} %copy.65) | copy-start | bytes 4718596
Sparse Core Ops, SparseCore 0:
  10.1 51.1 all-gather.8
  63.4 46.2 all-gather.12
  112.9 94.4 all-gather.10
  209.4 65.5 all-gather.14
  279.4 142.8 reduce-scatter.1
